TPU v7x, 32 devices: a whole 2x2x4 slice. The times are simulated.
32 devices in a mesh: seq: 8 (over z, x), hid: 4 (over y, core).
Axes of the slice: x: 2, y: 2, z: 4, core: 2. Of those that a mesh axis runs over, the one named last changes fastest.
Arguments:
- tokens: bfloat16 [1024, 4096], P('seq', 'hid'), may hold values from -6 to 6
- hidden_grad: bfloat16 [1024, 14336], P('seq', 'hid'), may hold values from -6 to 6
- gate_blocks: bfloat16 [4, 448, 128, 128], P('hid', 'seq'), may hold values from -0.125 to 0.125
- up_blocks: bfloat16 [4, 448, 128, 128], P('hid', 'seq'), may hold values from -0.125 to 0.125
- gate_rows: int32 [4, 448], P('hid'), may hold values from 0 to 31, as said below
- gate_cols: int32 [4, 448], P('hid'), may hold values from 0 to 27
- gate_count: int32 [4], P('hid'), may hold values from 56 to 448, as said below
- up_rows: int32 [4, 448], P('hid'), may hold values from 0 to 31, as said below
- up_cols: int32 [4, 448], P('hid'), may hold values from 0 to 27
- up_count: int32 [4], P('hid'), may hold values from 56 to 448, as said below
Outputs:
- hidden: bfloat16 [1024, 14336], P('seq', 'hid')
- input_grad: bfloat16 [1024, 4096], P('seq', 'hid')
- gate_block_grads: bfloat16 [4, 448, 128, 128], P('hid', 'seq')
- up_block_grads: bfloat16 [4, 448, 128, 128], P('hid', 'seq')
Inputs may be any that keep to these rules, and one draw needn't show every extreme that they name: For each panel, the pairs (gate_rows, gate_cols) over all 448 slots are distinct. `gate_count`: slots at or after a panel's count hold no block of the matrix. For each panel, the pairs (up_rows, up_cols) over all 448 slots are distinct. `up_count`: slots at or after a panel's count hold no block of the matrix.
All inputs are finite; a program needn't handle non-finite values.
Results may differ from a plain program's by a relative error of at most 0.018.
Values may be sent and summed in bfloat16 or wider, within the bound.
A program may use at most 192 MiB of HBM per device.

v0:
```python
import math
import jax
import jax.numpy as jnp
from jax import lax
from jax.sharding import PartitionSpec as P


def swapped(value, axis, stride):
    mask = 2**stride
    pairs = [(source, source ^ mask) for source in range(lax.axis_size(axis))]
    return lax.ppermute(value, axis, pairs)


def silu_parts(preact):
    sigma = jax.nn.sigmoid(preact)
    return (preact * sigma, sigma * (1.0 + preact * (1.0 - sigma)))


def place_split(products, placing, form):
    high_part = products.astype(jnp.bfloat16)
    rest_part = (products - high_part.astype(jnp.float32)).astype(jnp.bfloat16)
    table = placing.astype(jnp.bfloat16)
    placed = jnp.einsum(form, high_part, table, preferred_element_type=jnp.float32)
    return placed + jnp.einsum(form, rest_part, table, preferred_element_type=jnp.float32)


def project_slots(tiles, weights, rows, columns, live_count, group_size, trips, col_blocks):
    tok_rows = tiles.shape[0]
    block_size = tiles.shape[2]
    targets = jnp.arange(col_blocks)
    offsets = jnp.arange(group_size)

    def project_one_group(group_index, running):
        start = group_index * group_size
        chosen = lax.dynamic_slice_in_dim(weights, start, group_size, 0)
        row_ids = lax.dynamic_slice_in_dim(rows, start, group_size, 0)
        col_ids = lax.dynamic_slice_in_dim(columns, start, group_size, 0)
        active = start + offsets < live_count
        picked = jnp.take(tiles, row_ids, axis=1)
        products = jnp.einsum("tsk,skn->tsn", picked, chosen, preferred_element_type=jnp.float32)
        placing = (col_ids[:, None] == targets[None, :]) & active[:, None]
        return running + place_split(products, placing, "tsn,sc->tcn")

    initial = jnp.zeros((tok_rows, col_blocks, block_size), jnp.float32)
    return lax.fori_loop(0, trips, project_one_group, initial)


def return_slots(grad_tiles, weights, rows, columns, live_count, group_size, trips, row_blocks):
    tok_rows = grad_tiles.shape[0]
    block_size = grad_tiles.shape[2]
    targets = jnp.arange(row_blocks)
    offsets = jnp.arange(group_size)

    def return_one_group(group_index, running):
        start = group_index * group_size
        chosen = lax.dynamic_slice_in_dim(weights, start, group_size, 0)
        row_ids = lax.dynamic_slice_in_dim(rows, start, group_size, 0)
        col_ids = lax.dynamic_slice_in_dim(columns, start, group_size, 0)
        active = start + offsets < live_count
        picked = jnp.take(grad_tiles, col_ids, axis=1)
        products = jnp.einsum("tsn,skn->tsk", picked, chosen, preferred_element_type=jnp.float32)
        placing = (row_ids[:, None] == targets[None, :]) & active[:, None]
        return running + place_split(products, placing, "tsk,sr->trk")

    initial = jnp.zeros((tok_rows, row_blocks, block_size), jnp.float32)
    return lax.fori_loop(0, trips, return_one_group, initial)


def on_device(
    tokens,
    hidden_grad,
    gate_blocks,
    up_blocks,
    gate_rows,
    gate_cols,
    gate_count,
    up_rows,
    up_cols,
    up_count,
):
    gathered = lax.all_gather(tokens, "hid", axis=1, tiled=True)
    tok_rows = gathered.shape[0]
    block_size = gate_blocks.shape[2]
    row_blocks = gathered.shape[1] // block_size
    col_blocks = hidden_grad.shape[1] // block_size
    gate_all = lax.all_gather(gate_blocks, "seq", axis=1, tiled=True)
    up_all = lax.all_gather(up_blocks, "seq", axis=1, tiled=True)
    capacity = gate_all.shape[1]
    group_size = 32
    groups = capacity // group_size
    gate_live = gate_count[0]
    up_live = up_count[0]
    tiles = gathered.reshape(tok_rows, row_blocks, block_size)
    gate_pre = project_slots(
        tiles, gate_all[0], gate_rows[0], gate_cols[0], gate_live, group_size, groups, col_blocks
    )
    up_pre = project_slots(
        tiles, up_all[0], up_rows[0], up_cols[0], up_live, group_size, groups, col_blocks
    )
    activated, slope = silu_parts(gate_pre)
    hidden = (activated * up_pre).astype(jnp.bfloat16)
    upstream = hidden_grad.reshape(tok_rows, col_blocks, block_size).astype(jnp.float32)
    gate_grad = (upstream * up_pre * slope).astype(jnp.bfloat16)
    up_grad = (upstream * activated).astype(jnp.bfloat16)
    input_sum = return_slots(
        gate_grad,
        gate_all[0],
        gate_rows[0],
        gate_cols[0],
        gate_live,
        group_size,
        groups,
        row_blocks,
    )
    input_sum = input_sum + return_slots(
        up_grad, up_all[0], up_rows[0], up_cols[0], up_live, group_size, groups, row_blocks
    )
    input_grad = lax.psum_scatter(
        input_sum.reshape(tok_rows, row_blocks * block_size).astype(jnp.bfloat16),
        "hid",
        scatter_dimension=1,
        tiled=True,
    )
    seq_count = lax.axis_size("seq")
    position = lax.axis_index("seq")
    levels = seq_count.bit_length() - 1
    blk_dev = capacity // seq_count
    other_tiles, other_gate, other_up = swapped((tiles, gate_grad, up_grad), "seq", 0)
    both_tiles = jnp.concatenate([tiles, other_tiles], axis=0)
    both_gate = jnp.concatenate([gate_grad, other_gate], axis=0)
    both_up = jnp.concatenate([up_grad, other_up], axis=0)
    parity = position % 2
    owners = 2 * jnp.arange(seq_count // 2) + parity
    slot_ids = (owners[:, None] * blk_dev + jnp.arange(blk_dev)[None, :]).reshape(-1)
    stacked = []
    for rows, columns, live_count, grad_tiles in (
        (gate_rows[0], gate_cols[0], gate_live, both_gate),
        (up_rows[0], up_cols[0], up_live, both_up),
    ):
        row_ids = jnp.take(rows, slot_ids)
        col_ids = jnp.take(columns, slot_ids)
        picked_input = jnp.take(both_tiles, row_ids, axis=1)
        picked_grad = jnp.take(grad_tiles, col_ids, axis=1)
        block_term = jnp.einsum(
            "tsk,tsn->skn", picked_input, picked_grad, preferred_element_type=jnp.float32
        )
        stacked.append(block_term * (slot_ids < live_count).astype(jnp.float32)[:, None, None])
    current = jnp.stack(stacked, axis=1)
    current = current.reshape((seq_count // 2, blk_dev) + current.shape[1:])
    for level in range(1, levels):
        own_bit = position // 2**level % 2
        halves = current.reshape((current.shape[0] // 2, 2) + current.shape[1:])
        kept = lax.dynamic_index_in_dim(halves, own_bit, 1, keepdims=False)
        sent = lax.dynamic_index_in_dim(halves, 1 - own_bit, 1, keepdims=False)
        received = swapped(sent.astype(jnp.bfloat16), "seq", level)
        current = kept + received.astype(jnp.float32)
    summed = current[0]
    scale = 1.0 / math.sqrt(tok_rows * seq_count)
    gate_block_grads = (summed[:, 0] * scale).astype(jnp.bfloat16)[None]
    up_block_grads = (summed[:, 1] * scale).astype(jnp.bfloat16)[None]
    return (
        hidden.reshape(tok_rows, col_blocks * block_size),
        input_grad,
        gate_block_grads,
        up_block_grads,
    )


def solution(mesh):
    placed = (
        P("seq", "hid"),
        P("seq", "hid"),
        P("hid", "seq", None, None),
        P("hid", "seq", None, None),
        P("hid", None),
        P("hid", None),
        P("hid"),
        P("hid", None),
        P("hid", None),
        P("hid"),
    )
    return jax.shard_map(
        on_device,
        mesh=mesh,
        in_specs=placed,
        out_specs=(
            P("seq", "hid"),
            P("seq", "hid"),
            P("hid", "seq", None, None),
            P("hid", "seq", None, None),
        ),
        check_vma=False,
    )
```

profile of v0, /device:TPU:0, one launch (start us, length us, event | category | flops | bytes accessed | tf_op | source)
XLA Modules:
  0.0 1165.3 jit_solution(1844786483724718215)
XLA Ops:
  16.3 13.3 %all-gather.6.cloned.1.call-done = bf16[128,4096]{0,1:T(8,128)(2,1)} async-done(((bf16[128,1024]{0,1:T(8,128)(2,1)}), bf16[128,4096]{0,1:T(8,128)(2,1)}) %all-gather.6.cloned.1.call-update) | async-done | bytes 1048592 | tf_op jit(solution)/shard_map/all_gather | solution.py:81
  33.3 200.2 %all-gather.8.cloned.1.call-done = bf16[1,448,128,128]{3,2,0,1:T(8,128)(2,1)} async-done(((bf16[1,56,128,128]{3,2,0,1:T(8,128)(2,1)}), bf16[1,448,128,128]{3,2,0,1:T(8,128)(2,1)}) %all-gather.8.cloned.1.call-update) | async-done | bytes 14680080 | tf_op jit(solution)/shard_map/all_gather | solution.py:87
  233.5 192.3 %while.61 = (s32[]{:T(128)}, f32[128,28,128]{2,1,0:T(8,128)}, s32[448]{0:T(512)S(1)}, s32[]{:T(128)}, bf16[448,128,128]{2,1,0:T(8,128)(2,1)}, /*index=5*/s32[448...) while((s32[]{:T(128)}, f32[128,28,128]{2,1,0:T(8,128)}, ...), condition=%wide.region_3.5_spmd.clone, body=%wide.region_2.4_spmd.clone.sunk | while | flops 196940544 | bytes 19928416 | solution.py:45
  311.5 4.6 bitcast_add_fusion.9
  394.6 3.9 bitcast_add_fusion.9
  425.8 9.8 all-gather.4.cloned.1.call-done
  435.6 193.2 %while.60 = (s32[]{:T(128)}, f32[128,28,128]{2,1,0:T(8,128)}, s32[448]{0:T(512)S(1)}, s32[]{:T(128)}, bf16[448,128,128]{2,1,0:T(8,128)(2,1)}, /*index=5*/s32[448...) while((s32[]{:T(128)}, f32[128,28,128]{2,1,0:T(8,128)}, ...), condition=%wide.region_1.3_spmd.clone, body=%wide.region_0.2_spmd.clone.sunk | while | flops 196940544 | bytes 19928416 | solution.py:45
  569.6 3.8 bitcast_add_fusion.8
  628.8 6.5 multiply_convert_fusion.1
  645.1 9.4 gather_fusion.5
  654.5 9.2 gather_fusion.9
  665.3 9.2 gather_fusion.7
  678.0 9.1 gather_fusion.11
  687.2 18.4 %fusion.105 = f32[224,128,128]{2,1,0:T(8,128)} fusion(bf16[224,256,128]{2,1,0:T(8,128)(2,1)} %gather_fusion.7, pred[224]{0:T(512)(128)(4,1)S(1)} %get-tuple-element.961, bf16[224,256,128]{2,1,0:T(8,128)(2,1)} %gather_fusion.5, pred[224]{0:T(512)(128)(4,1)S(1)} %get-tuple-element.963, f32[224]{0:T(256)S(1)} %get-tuple-element.960), kind=kOutput, calls=%fused_computation.141 | convolution fusion | flops 1897398272 | bytes 44041536 | tf_op jit(solution)/shard_map/tsk,tsn->skn/dot_general | solution.py:144
  705.6 18.5 %fusion.110 = f32[224,128,128]{2,1,0:T(8,128)} fusion(bf16[224,256,128]{2,1,0:T(8,128)(2,1)} %gather_fusion.11, pred[224]{0:T(512)(128)(4,1)S(1)} %get-tuple-element.944, bf16[224,256,128]{2,1,0:T(8,128)(2,1)} %gather_fusion.9, pred[224]{0:T(512)(128)(4,1)S(1)} %get-tuple-element.941, f32[224]{0:T(256)S(1)} %get-tuple-element.959), kind=kOutput, calls=%fused_computation.142 | convolution fusion | flops 1897398272 | bytes 44041536 | tf_op jit(solution)/shard_map/tsk,tsn->skn/dot_general | solution.py:144
  724.1 10.1 fusion.115
  734.2 192.1 %while.62 = (s32[]{:T(128)}, f32[128,32,128]{2,1,0:T(8,128)}, s32[448]{0:T(512)S(1)}, s32[]{:T(128)}, bf16[448,128,128]{2,1,0:T(8,128)(2,1)}, /*index=5*/s32[448...) while((s32[]{:T(128)}, f32[128,32,128]{2,1,0:T(8,128)}, ...), condition=%wide.region_5.8_spmd.clone.clone, body=%wide.region_4.0_spmd.clone.clone.sunk | while | flops 205526272 | bytes 20976992 | solution.py:66
  757.1 3.9 bitcast_add_fusion.10
  770.9 3.9 bitcast_add_fusion.10
  784.7 3.9 bitcast_add_fusion.10
  798.5 3.9 bitcast_add_fusion.10
  812.2 3.9 bitcast_add_fusion.10
  826.0 3.9 bitcast_add_fusion.10
  839.8 3.9 bitcast_add_fusion.10
  853.5 3.9 bitcast_add_fusion.10
  867.3 3.9 bitcast_add_fusion.10
  881.1 3.9 bitcast_add_fusion.10
  894.8 3.9 bitcast_add_fusion.10
  908.6 3.9 bitcast_add_fusion.10
  922.4 3.9 bitcast_add_fusion.10
  926.2 8.6 fusion.90
  934.9 5.1 copy-done.7
  945.5 186.0 %while.63 = (s32[]{:T(128)}, f32[128,32,128]{2,1,0:T(8,128)}, s32[448]{0:T(512)}, s32[]{:T(128)}, bf16[448,128,128]{2,1,0:T(8,128)(2,1)}, /*index=5*/s32[448]{0:...) while((s32[]{:T(128)}, f32[128,32,128]{2,1,0:T(8,128)}, ...), condition=%wide.region_7.10_spmd.clone.clone, body=%wide.region_6.9_spmd.clone.clone.sunk | while | flops 205526272 | bytes 24647044 | solution.py:66
  967.5 3.9 bitcast_add_fusion.11
  980.9 3.9 bitcast_add_fusion.11
  994.2 3.9 bitcast_add_fusion.11
  1007.5 3.9 bitcast_add_fusion.11
  1020.9 3.9 bitcast_add_fusion.11
  1034.2 3.9 bitcast_add_fusion.11
  1047.5 3.9 bitcast_add_fusion.11
  1060.8 3.9 bitcast_add_fusion.11
  1074.2 3.9 bitcast_add_fusion.11
  1087.5 3.9 bitcast_add_fusion.11
  1100.8 3.9 bitcast_add_fusion.11
  1114.2 3.9 bitcast_add_fusion.11
  1127.5 3.9 bitcast_add_fusion.11
  1137.6 5.8 add_bitcast_fusion
  1146.2 12.6 %reduce-scatter.2.cloned.1.call-done = bf16[128,1024]{1,0:T(8,128)(2,1)} async-done(((bf16[128,4096]{1,0:T(8,128)(2,1)}), bf16[128,1024]{1,0:T(8,128)(2,1)}) %reduce-scatter.2.cloned.1.call-update) | async-done | bytes 262160 | tf_op jit(solution)/shard_map/reduce_scatter | solution.py:118
  (569 shorter events, 689.1 us)
Async XLA Ops:
  7.2 22.4 %all-gather.6.cloned.1.call-start = ((), (), s32[]{:S(2)}) async-start(), calls=%async_computation.2 | async-start | bytes 1310720 | tf_op jit(solution)/shard_map/all_gather | solution.py:81
  9.0 1.6 copy-start.9
  9.0 224.4 %all-gather.8.cloned.1.call-start = ((), (), s32[]{:S(2)}) async-start(), calls=%async_computation.3 | async-start | bytes 16515072 | tf_op jit(solution)/shard_map/all_gather | solution.py:87
  9.8 425.8 %all-gather.4.cloned.1.call-start = ((), (), s32[]{:S(2)}) async-start(), calls=%async_computation.1 | async-start | bytes 16515072 | tf_op jit(solution)/shard_map/all_gather | solution.py:86
  10.5 1148.3 %reduce-scatter.2.cloned.1.call-start = ((), (), s32[]{:S(2)}) async-start(), calls=%async_computation.4 | async-start | bytes 1310720 | tf_op jit(solution)/shard_map/reduce_scatter | solution.py:118
  10.6 3.7 copy-start.3
  12.8 220.6 %copy-start.2 = (s32[1,448]{1,0:T(1,128)S(1)}, s32[1,448]{1,0:T(1,128)}, u32[]{:S(2)}) copy-start(s32[1,448]{1,0:T(1,128)} %param.36) | copy-start | bytes 5380
  31.8 611.6 %collective-permute-start = (bf16[128,32,128]{2,0,1:T(8,128)(2,1)}, bf16[128,32,128]{2,0,1:T(8,128)(2,1)}, u32[]{:S(2)}, u32[]{:S(2)}) collective-permute-start(bf16[128,32,128]{2,0,1:T(8,128)(2,1)} %copy.98), channel_id=1, source_target_pairs={{0,4},{4,0},{8,12},{12,8},{16,20},{20,16},{24,28},{28,24},{1,5},{5... | collective-permute-start | bytes 3145736 | tf_op jit(solution)/shard_map/ppermute | solution.py:11
  233.5 202.1 %copy-start = (s32[1,448]{1,0:T(1,128)S(1)}, s32[1,448]{1,0:T(1,128)}, u32[]{:S(2)}) copy-start(s32[1,448]{1,0:T(1,128)} %param.33) | copy-start | bytes 5380
  233.5 202.1 %copy-start.1 = (s32[1,448]{1,0:T(1,128)S(1)}, s32[1,448]{1,0:T(1,128)}, u32[]{:S(2)}) copy-start(s32[1,448]{1,0:T(1,128)} %param.32) | copy-start | bytes 5380
  635.3 41.4 %copy-start.4 = (bf16[128,28,128]{2,0,1:T(8,128)(2,1)}, bf16[128,28,128]{2,0,1:T(8,128)(2,1)S(1)}, u32[]{:S(2)}) copy-start(bf16[128,28,128]{2,0,1:T(8,128)(2,1)S(1)} %get-tuple-element.1284) | copy-start | bytes 2752516
  635.3 28.4 %collective-permute-start.1 = (bf16[128,28,128]{2,0,1:T(8,128)(2,1)}, bf16[128,28,128]{2,0,1:T(8,128)(2,1)}, u32[]{:S(2)}, u32[]{:S(2)}) collective-permute-start(bf16[128,28,128]{2,0,1:T(8,128)(2,1)} %get-tuple-element.1251), channel_id=1, source_target_pairs={{0,4},{4,0},{8,12},{12,8},{16,20},{20,16},{24,28},{28,24},{1,5},{5... | collective-permute-start | bytes 2752520 | tf_op jit(solution)/shard_map/ppermute | solution.py:11
  635.9 40.8 %collective-permute-start.2 = (bf16[128,28,128]{2,0,1:T(8,128)(2,1)S(1)}, bf16[128,28,128]{2,0,1:T(8,128)(2,1)}, u32[]{:S(2)}, u32[]{:S(2)}) collective-permute-start(bf16[128,28,128]{2,0,1:T(8,128)(2,1)S(1)} %get-tuple-element.1284), channel_id=1, source_target_pairs={{0,4},{4,0},{8,12},{12,8},{16,20},{20,16},{24,28},{28,24},{1,5},{5... | collective-permute-start | bytes 2752520 | tf_op jit(solution)/shard_map/ppermute | solution.py:11
  734.2 192.1 %collective-permute-start.3 = (bf16[2,56,2,128,128]{4,3,1,2,0:T(8,128)(2,1)}, bf16[2,56,2,128,128]{4,3,1,2,0:T(8,128)(2,1)}, u32[]{:S(2)}, u32[]{:S(2)}) collective-permute-start(bf16[2,56,2,128,128]{4,3,1,2,0:T(8,128)(2,1)} %fusion.115), channel_id=1, source_target_pairs={{0,8},{4,12},{8,0},{12,4},{16,24},{20,28},{24,16},{28,20},{1,9},{5... | collective-permute-start | bytes 22020104 | tf_op jit(solution)/shard_map/ppermute | solution.py:11
  934.9 5.1 copy-start.7
  940.0 5.5 copy-start.5
  942.7 194.9 %collective-permute-start.4 = (bf16[1,56,2,128,128]{4,3,1,2,0:T(8,128)(2,1)}, bf16[1,56,2,128,128]{4,3,1,2,0:T(8,128)(2,1)}, u32[]{:S(2)}, u32[]{:S(2)}) collective-permute-start(bf16[1,56,2,128,128]{4,3,1,2,0:T(8,128)(2,1)} %dynamic-slice_convert_fusion), channel_id=1, source_target_pairs={{0,16},{4,20},{8,24},{12,28},{16,0},{20,4},{24,8},{28,12},{1,17},{... | collective-permute-start | bytes 11010056 | tf_op jit(solution)/shard_map/ppermute | solution.py:11
  954.9 3.3 copy-start.6
  967.5 3.9 copy-start.6
  980.9 3.9 copy-start.6
  994.2 3.9 copy-start.6
  1007.5 3.9 copy-start.6
  1020.9 3.9 copy-start.6
  1034.2 3.9 copy-start.6
  1047.5 3.9 copy-start.6
  1060.8 3.9 copy-start.6
  1074.2 3.9 copy-start.6
  1087.5 3.9 copy-start.6
  1100.8 3.9 copy-start.6
  1114.2 3.9 copy-start.6
  1127.5 3.9 copy-start.6
  1134.1 1.5 copy-start.8
Sparse Core Ops, SparseCore 0:
  10.1 19.4 all-gather.5
  31.8 201.6 all-gather.7
  235.7 199.8 all-gather.3
  1135.7 23.0 reduce-scatter.1
where the time goes:
time: 1170 us
  matrix products  462 us (39%)
  local copies, waits for them, and re-layouts  359 us (31%)
  waiting for transfers between devices  239 us (20%)
  other arithmetic  82.2 us (7%)
  between operations  15.4 us (1%)
    dot_general x56, matrix products, place_split(): jnp.einsum(form, rest_part, table, preferred_element_type=jnp.float32)  213 us
    all_gather x1, waiting for transfers between devices, on_device(): up_all = lax.all_gather(up_blocks, 'seq', axis=1, tiled=True)  200 us
    convert_element_type x56, local copies, waits for them, and re-layouts, place_split(): rest_part = (products - high_part.astype(jnp.float32)).astype(jnp.bfloat16)  95.1 us
    convert_element_type x56, local copies, waits for them, and re-layouts, place_split(): high_part = products.astype(jnp.bfloat16)  95 us
    dot_general x56, matrix products, place_split(): jnp.einsum(form, high_part, table, preferred_element_type=jnp.float32)  91.5 us
    dot_general x28, matrix products, return_one_group(): jnp.einsum('tsn,skn->tsk', picked, chosen, preferred_element_type=jnp.flo...  60.6 us
    dot_general x28, matrix products, project_one_group(): jnp.einsum('tsk,skn->tsn', picked, chosen, preferred_element_type=jnp.flo...  59.6 us
    gather x28, local copies, waits for them, and re-layouts, project_one_group(): picked = jnp.take(tiles, row_ids, axis=1)  55.3 us
  transfers between devices with their start and end apart: 9, of which 5 were waited for; matrix products, arithmetic and copies ran while one was open for 71% of the time, Pallas kernels for 0%

commit v1 on v0

--- a/solution.py
+++ b/solution.py
@@ -83,8 +83,11 @@
     block_size = gate_blocks.shape[2]
     row_blocks = gathered.shape[1] // block_size
     col_blocks = hidden_grad.shape[1] // block_size
-    gate_all = lax.all_gather(gate_blocks, "seq", axis=1, tiled=True)
-    up_all = lax.all_gather(up_blocks, "seq", axis=1, tiled=True)
+    gate_all, up_all = jnp.split(
+        lax.all_gather(jnp.concatenate([gate_blocks, up_blocks], 0), "seq", axis=1, tiled=True),
+        [gate_blocks.shape[0]],
+        0,
+    )
     capacity = gate_all.shape[1]
     group_size = 32
     groups = capacity // group_size

time: 1170 us -> 1560 us (1.33)
  waiting for transfers between devices: 239 us -> 599 us
  local copies, waits for them, and re-layouts: 359 us -> 380 us
    all_gather x2 -> x1, waiting for transfers between devices: 210 us -> 575 us  [on_device(): lax.all_gather(jnp.concatenate([gate_blocks, up_blocks], 0), 'seq', axis=...]
    squeeze x0 -> x1, local copies, waits for them, and re-layouts: none -> 22.2 us  [on_device(): gate_all[0]]
  transfers between devices with their start and end apart: 9 -> 8, of which waited for: 5 -> 4; matrix products, arithmetic and copies ran while one was open for 71% -> 55% of each run, Pallas kernels for 0% -> 0%
where the time goes in v1:
time: 1560 us; the launch traced here: 1550 us
  waiting for transfers between devices  599 us (38%)
  matrix products  461 us (30%)
  local copies, waits for them, and re-layouts  380 us (24%)
  other arithmetic  86.4 us (6%)
    all_gather x1, waiting for transfers between devices, on_device(): lax.all_gather(jnp.concatenate([gate_blocks, up_blocks], 0), 'seq', axis=...  575 us
    dot_general x56, matrix products, place_split(): jnp.einsum(form, rest_part, table, preferred_element_type=jnp.float32)  213 us
    convert_element_type x56, local copies, waits for them, and re-layouts, place_split(): high_part = products.astype(jnp.bfloat16)  94.1 us
    convert_element_type x56, local copies, waits for them, and re-layouts, place_split(): rest_part = (products - high_part.astype(jnp.float32)).astype(jnp.bfloat16)  94.1 us
    dot_general x56, matrix products, place_split(): jnp.einsum(form, high_part, table, preferred_element_type=jnp.float32)  91.2 us
    dot_general x28, matrix products, return_one_group(): jnp.einsum('tsn,skn->tsk', picked, chosen, preferred_element_type=jnp.flo...  60.6 us
    dot_general x28, matrix products, project_one_group(): jnp.einsum('tsk,skn->tsn', picked, chosen, preferred_element_type=jnp.flo...  59.5 us
    gather x28, local copies, waits for them, and re-layouts, project_one_group(): picked = jnp.take(tiles, row_ids, axis=1)  55.3 us
  transfers between devices with their start and end apart: 8, of which 4 were waited for; matrix products, arithmetic and copies ran while one was open for 55% of the time, Pallas kernels for 0%

profile of v1, /device:TPU:0, one launch (start us, length us, event | category | flops | bytes accessed | tf_op | source)
XLA Modules:
  0.0 1551.3 jit_solution(13579429911602914801)
XLA Ops:
  9.1 4.2 pad_maximum_fusion
  20.1 9.5 all-gather.5.cloned.1.call-done
  33.3 575.1 %all-gather.3.cloned.1.call-done = bf16[2,448,128,128]{3,2,1,0:T(8,128)(2,1)} async-done(((bf16[2,56,128,128]{3,2,1,0:T(8,128)(2,1)}), bf16[2,448,128,128]{3,2,1,0:T(8,128)(2,1)}) %all-gather.3.cloned.1.call-update) | async-done | bytes 29360144 | tf_op jit(solution)/shard_map/all_gather | solution.py:87
  608.4 22.2 %slice_bitcast_fusion.1 = (bf16[448,128,128]{2,1,0:T(8,128)(2,1)}, bf16[448,128,128]{2,1,0:T(8,128)(2,1)}) fusion(bf16[2,448,128,128]{3,2,1,0:T(8,128)(2,1)} %all-gather.3.cloned.1.call-done), kind=kLoop, calls=%fused_computation.125 | loop fusion | bytes 58720256 | tf_op jit(solution)/shard_map/squeeze | solution.py:98
  630.7 190.1 %while.61 = (s32[]{:T(128)}, f32[128,28,128]{2,1,0:T(8,128)}, s32[448]{0:T(512)S(1)}, s32[]{:T(128)}, bf16[448,128,128]{2,1,0:T(8,128)(2,1)}, /*index=5*/s32[448...) while((s32[]{:T(128)}, f32[128,28,128]{2,1,0:T(8,128)}, ...), condition=%wide.region_3.5_spmd.clone, body=%wide.region_2.4_spmd.clone.sunk | while | flops 196940544 | bytes 19928416 | solution.py:45
  820.8 193.0 %while.60 = (s32[]{:T(128)}, f32[128,28,128]{2,1,0:T(8,128)}, s32[448]{0:T(512)S(1)}, s32[]{:T(128)}, bf16[448,128,128]{2,1,0:T(8,128)(2,1)}, /*index=5*/s32[448...) while((s32[]{:T(128)}, f32[128,28,128]{2,1,0:T(8,128)}, ...), condition=%wide.region_1.3_spmd.clone, body=%wide.region_0.2_spmd.clone.sunk | while | flops 196940544 | bytes 19928416 | solution.py:45
  843.9 3.9 bitcast_add_fusion.8
  857.7 3.9 bitcast_add_fusion.8
  871.6 3.9 bitcast_add_fusion.8
  885.4 3.9 bitcast_add_fusion.8
  899.2 3.9 bitcast_add_fusion.8
  913.1 3.9 bitcast_add_fusion.8
  926.9 3.9 bitcast_add_fusion.8
  940.7 3.9 bitcast_add_fusion.8
  954.6 3.9 bitcast_add_fusion.8
  968.4 3.9 bitcast_add_fusion.8
  982.2 3.9 bitcast_add_fusion.8
  996.1 3.9 bitcast_add_fusion.8
  1009.9 3.9 bitcast_add_fusion.8
  1013.8 6.5 multiply_convert_fusion.1
  1030.1 9.3 gather_fusion.5
  1039.4 9.2 gather_fusion.9
  1050.2 9.2 gather_fusion.7
  1063.8 9.1 gather_fusion.11
  1073.0 18.5 %fusion.105 = f32[224,128,128]{2,1,0:T(8,128)} fusion(bf16[224,256,128]{2,1,0:T(8,128)(2,1)} %gather_fusion.7, pred[224]{0:T(512)(128)(4,1)S(1)} %get-tuple-element.945, bf16[224,256,128]{2,1,0:T(8,128)(2,1)} %gather_fusion.5, pred[224]{0:T(512)(128)(4,1)S(1)} %get-tuple-element.947, f32[224]{0:T(256)S(1)} %get-tuple-element.944), kind=kOutput, calls=%fused_computation.143 | convolution fusion | flops 1897398272 | bytes 44041536 | tf_op jit(solution)/shard_map/tsk,tsn->skn/dot_general | solution.py:147
  1091.5 18.5 %fusion.110 = f32[224,128,128]{2,1,0:T(8,128)} fusion(bf16[224,256,128]{2,1,0:T(8,128)(2,1)} %gather_fusion.11, pred[224]{0:T(512)(128)(4,1)S(1)} %get-tuple-element.926, bf16[224,256,128]{2,1,0:T(8,128)(2,1)} %gather_fusion.9, pred[224]{0:T(512)(128)(4,1)S(1)} %get-tuple-element.923, f32[224]{0:T(256)S(1)} %get-tuple-element.943), kind=kOutput, calls=%fused_computation.144 | convolution fusion | flops 1897398272 | bytes 44041536 | tf_op jit(solution)/shard_map/tsk,tsn->skn/dot_general | solution.py:147
  1110.0 10.1 fusion.115
  1121.6 192.0 %while.62 = (s32[]{:T(128)}, f32[128,32,128]{2,1,0:T(8,128)}, s32[448]{0:T(512)S(1)}, s32[]{:T(128)}, bf16[448,128,128]{2,1,0:T(8,128)(2,1)}, /*index=5*/s32[448...) while((s32[]{:T(128)}, f32[128,32,128]{2,1,0:T(8,128)}, ...), condition=%wide.region_5.8_spmd.clone.clone, body=%wide.region_4.0_spmd.clone.clone.sunk | while | flops 205526272 | bytes 20976992 | solution.py:66
  1144.6 3.9 bitcast_add_fusion.10
  1158.3 3.9 bitcast_add_fusion.10
  1313.5 8.6 fusion.90
  1322.1 5.2 copy-done.7
  1332.4 185.9 %while.63 = (s32[]{:T(128)}, f32[128,32,128]{2,1,0:T(8,128)}, s32[448]{0:T(512)}, s32[]{:T(128)}, bf16[448,128,128]{2,1,0:T(8,128)(2,1)}, /*index=5*/s32[448]{0:...) while((s32[]{:T(128)}, f32[128,32,128]{2,1,0:T(8,128)}, ...), condition=%wide.region_7.10_spmd.clone.clone, body=%wide.region_6.9_spmd.clone.clone.sunk | while | flops 205526272 | bytes 24647044 | solution.py:66
  1354.5 3.9 bitcast_add_fusion.11
  1367.8 3.9 bitcast_add_fusion.11
  1381.1 3.9 bitcast_add_fusion.11
  1394.4 3.9 bitcast_add_fusion.11
  1407.8 3.9 bitcast_add_fusion.11
  1421.1 3.9 bitcast_add_fusion.11
  1434.4 3.9 bitcast_add_fusion.11
  1447.7 3.9 bitcast_add_fusion.11
  1461.1 3.9 bitcast_add_fusion.11
  1474.4 3.9 bitcast_add_fusion.11
  1487.7 3.9 bitcast_add_fusion.11
  1501.0 3.9 bitcast_add_fusion.11
  1514.3 3.9 bitcast_add_fusion.11
  1524.5 5.9 add_bitcast_fusion
  1533.2 11.6 reduce-scatter.2.cloned.1.call-done
  (568 shorter events, 692.5 us)
Async XLA Ops:
  7.2 22.4 %all-gather.5.cloned.1.call-start = ((), (), s32[]{:S(2)}) async-start(), calls=%async_computation.2 | async-start | bytes 1310720 | tf_op jit(solution)/shard_map/all_gather | solution.py:81
  9.0 599.4 %all-gather.3.cloned.1.call-start = ((), (), s32[]{:S(2)}) async-start(), calls=%async_computation.1 | async-start | bytes 33030144 | tf_op jit(solution)/shard_map/all_gather | solution.py:87
  13.2 1.2 copy-start.9
  13.2 4.9 copy-start.3
  13.3 1531.5 %reduce-scatter.2.cloned.1.call-start = ((), (), s32[]{:S(2)}) async-start(), calls=%async_computation.3 | async-start | bytes 1310720 | tf_op jit(solution)/shard_map/reduce_scatter | solution.py:121
  31.8 598.8 %copy-start.2 = (s32[1,448]{1,0:T(1,128)S(1)}, s32[1,448]{1,0:T(1,128)}, u32[]{:S(2)}) copy-start(s32[1,448]{1,0:T(1,128)} %param.36) | copy-start | bytes 5380
  31.8 996.6 %collective-permute-start = (bf16[128,32,128]{2,0,1:T(8,128)(2,1)}, bf16[128,32,128]{2,0,1:T(8,128)(2,1)}, u32[]{:S(2)}, u32[]{:S(2)}) collective-permute-start(bf16[128,32,128]{2,0,1:T(8,128)(2,1)} %copy.68), channel_id=1, source_target_pairs={{0,4},{4,0},{8,12},{12,8},{16,20},{20,16},{24,28},{28,24},{1,5},{5... | collective-permute-start | bytes 3145736 | tf_op jit(solution)/shard_map/ppermute | solution.py:11
  630.6 190.1 %copy-start = (s32[1,448]{1,0:T(1,128)S(1)}, s32[1,448]{1,0:T(1,128)}, u32[]{:S(2)}) copy-start(s32[1,448]{1,0:T(1,128)} %param.33) | copy-start | bytes 5380
  630.7 190.1 %copy-start.1 = (s32[1,448]{1,0:T(1,128)S(1)}, s32[1,448]{1,0:T(1,128)}, u32[]{:S(2)}) copy-start(s32[1,448]{1,0:T(1,128)} %param.32) | copy-start | bytes 5380
  1020.3 42.2 %copy-start.4 = (bf16[128,28,128]{2,0,1:T(8,128)(2,1)}, bf16[128,28,128]{2,0,1:T(8,128)(2,1)S(1)}, u32[]{:S(2)}) copy-start(bf16[128,28,128]{2,0,1:T(8,128)(2,1)S(1)} %get-tuple-element.1268) | copy-start | bytes 2752516
  1020.3 28.3 %collective-permute-start.1 = (bf16[128,28,128]{2,0,1:T(8,128)(2,1)}, bf16[128,28,128]{2,0,1:T(8,128)(2,1)}, u32[]{:S(2)}, u32[]{:S(2)}) collective-permute-start(bf16[128,28,128]{2,0,1:T(8,128)(2,1)} %get-tuple-element.1235), channel_id=1, source_target_pairs={{0,4},{4,0},{8,12},{12,8},{16,20},{20,16},{24,28},{28,24},{1,5},{5... | collective-permute-start | bytes 2752520 | tf_op jit(solution)/shard_map/ppermute | solution.py:11
  1021.8 40.7 %collective-permute-start.2 = (bf16[128,28,128]{2,0,1:T(8,128)(2,1)S(1)}, bf16[128,28,128]{2,0,1:T(8,128)(2,1)}, u32[]{:S(2)}, u32[]{:S(2)}) collective-permute-start(bf16[128,28,128]{2,0,1:T(8,128)(2,1)S(1)} %get-tuple-element.1268), channel_id=1, source_target_pairs={{0,4},{4,0},{8,12},{12,8},{16,20},{20,16},{24,28},{28,24},{1,5},{5... | collective-permute-start | bytes 2752520 | tf_op jit(solution)/shard_map/ppermute | solution.py:11
  1120.0 193.5 %collective-permute-start.3 = (bf16[2,56,2,128,128]{4,3,1,2,0:T(8,128)(2,1)}, bf16[2,56,2,128,128]{4,3,1,2,0:T(8,128)(2,1)}, u32[]{:S(2)}, u32[]{:S(2)}) collective-permute-start(bf16[2,56,2,128,128]{4,3,1,2,0:T(8,128)(2,1)} %fusion.115), channel_id=1, source_target_pairs={{0,8},{4,12},{8,0},{12,4},{16,24},{20,28},{24,16},{28,20},{1,9},{5... | collective-permute-start | bytes 22020104 | tf_op jit(solution)/shard_map/ppermute | solution.py:11
  1322.1 5.2 copy-start.7
  1327.3 5.1 copy-start.5
  1330.0 194.5 %collective-permute-start.4 = (bf16[1,56,2,128,128]{4,3,1,2,0:T(8,128)(2,1)}, bf16[1,56,2,128,128]{4,3,1,2,0:T(8,128)(2,1)}, u32[]{:S(2)}, u32[]{:S(2)}) collective-permute-start(bf16[1,56,2,128,128]{4,3,1,2,0:T(8,128)(2,1)} %dynamic-slice_convert_fusion), channel_id=1, source_target_pairs={{0,16},{4,20},{8,24},{12,28},{16,0},{20,4},{24,8},{28,12},{1,17},{... | collective-permute-start | bytes 11010056 | tf_op jit(solution)/shard_map/ppermute | solution.py:11
  1341.8 3.2 copy-start.6
  1354.5 3.9 copy-start.6
  1367.8 3.9 copy-start.6
  1381.1 3.9 copy-start.6
  1394.4 3.9 copy-start.6
  1407.8 3.9 copy-start.6
  1421.1 3.9 copy-start.6
  1434.4 3.9 copy-start.6
  1447.7 3.9 copy-start.6
  1461.0 3.9 copy-start.6
  1474.4 3.9 copy-start.6
  1487.7 3.9 copy-start.6
  1501.0 3.9 copy-start.6
  1514.3 3.9 copy-start.6
  1518.3 4.3 copy-start.8
Sparse Core Ops, SparseCore 0:
  10.1 19.4 all-gather.4
  31.1 577.2 all-gather.2
  1522.7 22.0 reduce-scatter.1
